TPU v7x, 32 devices: a whole 2x2x4 slice. The times are simulated.
32 devices in a mesh: ctx: 4 (over z), exp: 4 (over y, x), head: 2 (over core).
Axes of the slice: x: 2, y: 2, z: 4, core: 2. Of those that a mesh axis runs over, the one named last changes fastest.
Arguments:
- queries: bfloat16 [2048, 2048], P(('ctx', 'exp'), 'head'), may hold values from -6 to 6
- keys: bfloat16 [2048, 256], P(('ctx', 'exp'), 'head'), may hold values from -6 to 6
- values: bfloat16 [2048, 256], P(('ctx', 'exp'), 'head'), may hold values from -12 to 12
- residual: bfloat16 [2048, 2880], P(('ctx', 'exp', 'head')), may hold values from -48 to 48
- out_projection: bfloat16 [2048, 2880], P('head', 'exp'), may hold values from -0.125 to 0.125
- norm_gain: float32 [2880], replicated, may hold values from 0.25 to 1.75
- route_ids: int32 [2048, 4], P(('ctx', 'exp', 'head')), may hold values from 0 to 7, all different within a row; in each aligned block of 64 rows (0 to 63, 64 to 127, ...) at most 64 rows name the same one
- route_weights: float32 [2048, 4], P(('ctx', 'exp', 'head')), may hold values from 0.05 to 1
- w_gate: bfloat16 [8, 2880, 1536], P(('ctx', 'head'), None, 'exp'), may hold values from -0.109375 to 0.109375
- w_up: bfloat16 [8, 2880, 1536], P(('ctx', 'head'), None, 'exp'), may hold values from -0.109375 to 0.109375
- w_down: bfloat16 [8, 1536, 2880], P(('ctx', 'head'), 'exp'), may hold values from -0.15625 to 0.15625
Outputs:
- mixed: bfloat16 [2048, 2880], P(('ctx', 'exp', 'head'))
Inputs may be any that keep to these rules, and one draw needn't show every extreme that they name: `route_ids`: each row names 4 different experts. In the rows of one device (aligned blocks of 64 rows) no expert is named by more than 64 rows, a bound that some block reaches.
All inputs are finite; a program needn't handle non-finite values.
Results may differ from a plain program's by a relative error of at most 0.0037.
Values may be sent and summed in bfloat16 or wider, within the bound.
No kernel may reach another device: no remote copies, remote signals or barrier semaphores. Data moves between devices by JAX's collectives and lax.ppermute only.
A program may use at most 128 MiB of HBM per device.

v0:
```python
import jax
import jax.numpy as jnp
from jax import lax
from jax.sharding import PartitionSpec as P

D = 2880
QUERY_HEADS = 32
KEY_VALUE_HEADS = 4
HEAD_DIMENSION = 64
BAND_WIDTH_KEYS = 128
TOP = 4
EPSILON = 1e-05
SLOPE = 1.702


def from_behind(x, axis, by):
    devices = lax.axis_size(axis)
    pairs = [(i, i + by) for i in range(devices) if 0 <= i + by < devices]
    return lax.ppermute(x, axis, pairs)


def attend_band(
    queries, concatenated_keys, concatenated_values, window, head_size, group, anchor_position
):
    tokens = queries.shape[0]
    block = min(tokens, 512)
    count = tokens // block
    heads = queries.shape[1] // head_size
    kv_heads = heads // group
    scale = head_size ** (-0.5)

    def one_block(index):
        begin = index * block
        query_part = queries.reshape(block, kv_heads, group, head_size)
        key_part = concatenated_keys.reshape(block + window, kv_heads, head_size)
        value_part = concatenated_values.reshape(block + window, kv_heads, head_size)
        scores = (
            jnp.einsum("qgjd,kgd->gjqk", query_part, key_part, preferred_element_type=jnp.float32)
            * scale
        )
        query_pos = anchor_position + begin + jnp.arange(block, dtype=jnp.int32)
        key_pos = anchor_position - window + begin + jnp.arange(block + window, dtype=jnp.int32)
        distance = query_pos[:, None] - key_pos[None, :]
        allowed = (distance >= 0) & (distance < window) & (key_pos[None, :] >= 0)
        scores = jnp.where(allowed, scores, -jnp.inf)
        highest = jnp.max(scores, axis=-1, keepdims=True)
        weights = jnp.exp(scores - highest)
        weights = (weights / jnp.sum(weights, axis=-1, keepdims=True)).astype(jnp.bfloat16)
        result = jnp.einsum(
            "gjqk,kgd->qgjd", weights, value_part, preferred_element_type=jnp.float32
        )
        return result.astype(jnp.bfloat16).reshape(block, heads * head_size)

    outputs = lax.map(one_block, jnp.arange(count, dtype=jnp.int32))
    return outputs.reshape(tokens, heads * head_size)


def expert_rows(inputs, gate_slice, up_slice, down_slice):
    gate = jnp.dot(inputs, gate_slice, preferred_element_type=jnp.float32)
    upward = jnp.dot(inputs, up_slice, preferred_element_type=jnp.float32)
    active = ((upward + 1.0) * gate * jax.nn.sigmoid(SLOPE * gate)).astype(jnp.bfloat16)
    return jnp.dot(active, down_slice, preferred_element_type=jnp.float32)


def local(
    queries,
    keys,
    values,
    residual,
    out_projection,
    norm_gain,
    route_ids,
    route_weights,
    w_gate,
    w_up,
    w_down,
):
    tokens = queries.shape[0]
    key_band_extent = keys.shape[1]
    stacked = jnp.concatenate([keys, values], axis=1)
    prior = from_behind(stacked, ("ctx", "exp"), 1)
    joined_heads = jnp.concatenate([prior, stacked], axis=0)
    anchor_position = lax.axis_index(("ctx", "exp")) * tokens
    attended_rows = attend_band(
        queries,
        joined_heads[:, :key_band_extent],
        joined_heads[:, key_band_extent:],
        BAND_WIDTH_KEYS,
        HEAD_DIMENSION,
        QUERY_HEADS // KEY_VALUE_HEADS,
        anchor_position,
    )
    partial_sum = jnp.dot(
        attended_rows,
        lax.all_gather(out_projection, "exp", axis=1, tiled=True),
        preferred_element_type=jnp.float32,
    )
    attn_out = lax.psum_scatter(partial_sum, "head", scatter_dimension=0, tiled=True)
    hidden_state = residual.astype(jnp.float32) + attn_out
    mean_square = jnp.mean(hidden_state * hidden_state, axis=1, keepdims=True)
    normed = (hidden_state * lax.rsqrt(mean_square + EPSILON) * norm_gain[None, :]).astype(
        jnp.bfloat16
    )
    local_rows = normed.shape[0]
    experts = lax.axis_size("ctx") * lax.axis_size("head")
    capacity = max(2, TOP * tokens // experts)
    flat_ids = route_ids.reshape(-1)
    one_hot = (flat_ids[:, None] == jnp.arange(experts, dtype=jnp.int32)[None, :]).astype(jnp.int32)
    earlier = jnp.cumsum(one_hot, axis=0) - one_hot
    rank = jnp.sum(earlier * one_hot, axis=1)
    slot = flat_ids * capacity + rank
    outgoing = (
        jnp.zeros((experts * capacity, D), jnp.bfloat16)
        .at[slot]
        .set(jnp.repeat(normed, TOP, axis=0))
    )
    outgoing = outgoing.reshape(experts, capacity, D)
    arrived = lax.all_to_all(outgoing, ("ctx", "head"), split_axis=0, concat_axis=0, tiled=True)
    pooled = lax.all_gather(arrived, "exp", axis=0, tiled=True)
    partial_rows = expert_rows(
        pooled.reshape(experts * lax.axis_size("exp") * capacity, D), w_gate[0], w_up[0], w_down[0]
    )
    summed = lax.psum_scatter(
        partial_rows.reshape(experts * lax.axis_size("exp"), capacity, D),
        "exp",
        scatter_dimension=0,
        tiled=True,
    ).astype(jnp.bfloat16)
    returned = lax.all_to_all(summed, ("ctx", "head"), split_axis=0, concat_axis=0, tiled=True)
    flat_back = returned.reshape(experts * capacity, D)
    picked = flat_back[slot].astype(jnp.float32).reshape(local_rows, TOP, D)
    moe = jnp.sum(picked * route_weights[:, :, None], axis=1)
    return (hidden_state + moe).astype(jnp.bfloat16)


def solution(mesh):
    return jax.shard_map(
        local,
        mesh=mesh,
        in_specs=(
            P(("ctx", "exp"), "head"),
            P(("ctx", "exp"), "head"),
            P(("ctx", "exp"), "head"),
            P(("ctx", "exp", "head"), None),
            P("head", "exp"),
            P(),
            P(("ctx", "exp", "head"), None),
            P(("ctx", "exp", "head"), None),
            P(("ctx", "head"), None, "exp"),
            P(("ctx", "head"), None, "exp"),
            P(("ctx", "head"), "exp", None),
        ),
        out_specs=P(("ctx", "exp", "head"), None),
        check_vma=False,
    )
```

profile of v0, /device:TPU:0, one launch (start us, length us, event | category | flops | bytes accessed | tf_op | source)
XLA Modules:
  0.0 637.0 jit_solution(17359367700430694004)
XLA Ops:
  6.5 0.7 all-gather.3.cloned.1.call-update
  7.3 0.8 constant_dynamic-update-slice_fusion.1
  8.1 0.8 constant_dynamic-update-slice_fusion
  8.8 4.9 collective-permute-start
  13.9 1.1 copy.27
  15.0 0.6 collective-permute-done
  15.8 0.8 fusion.26
  16.6 1.1 convolution_convert_fusion
  17.7 61.0 %all-gather.3.cloned.1.call-done = bf16[1024,2880]{0,1:T(8,128)(2,1)} async-done(((bf16[1024,720]{0,1:T(8,128)(2,1)}), bf16[1024,2880]{0,1:T(8,128)(2,1)}) %all-gather.3.cloned.1.call-update) | async-done | bytes 5898256 | tf_op jit(solution)/shard_map/all_gather | solution.py:95
  78.7 6.0 fusion.27
  85.1 0.6 reduce-window.6
  85.7 0.2 slice_reduce_fusion
  86.2 7.6 %reduce-scatter.3.cloned.1.call-done = f32[64,2880]{1,0:T(8,128)} async-done(((f32[128,2880]{1,0:T(8,128)}), f32[64,2880]{1,0:T(8,128)}) %reduce-scatter.3.cloned.1.call-update) | async-done | bytes 737296 | tf_op jit(solution)/shard_map/reduce_scatter | solution.py:98
  93.8 1.3 multiply_reduce_fusion.1
  95.2 1.3 multiply_convert_fusion.1
  96.4 1.5 broadcast_in_dim.38
  98.0 3.6 reshape.129
  101.5 5.6 scatter_custom_fusion
  107.1 73.8 %all_to_all.10 = bf16[8,64,2880]{2,1,0:T(8,128)(2,1)} all-to-all(bf16[8,64,2880]{2,1,0:T(8,128)(2,1)} %bitcast.60), channel_id=1, replica_groups=mesh['ctx'=4,'exp'=4,'head'=2] {'ctx','head'}, dimensions={0} | all-to-all | bytes 5898240 | tf_op jit(solution)/shard_map/all_to_all | solution.py:118
  180.9 0.2 reduce-scatter.5.cloned.1.call-start
  181.1 116.8 %all-gather.5.cloned.1.call-done = bf16[32,64,2880]{2,1,0:T(8,128)(2,1)} async-done(((bf16[8,64,2880]{2,1,0:T(8,128)(2,1)}), bf16[32,64,2880]{2,1,0:T(8,128)(2,1)}) %all-gather.5.cloned.1.call-update) | async-done | bytes 11796496 | tf_op jit(solution)/shard_map/all_gather | solution.py:119
  298.0 10.6 %fusion.3 = f32[2048,384]{1,0:T(8,128)S(1)} fusion(bf16[2048,2880]{1,0:T(8,128)(2,1)} %bitcast.71, bf16[1,2880,384]{2,1,0:T(8,128)(2,1)} %param.19), kind=kOutput, calls=%fused_computation.7 | convolution fusion | flops 4529848320 | bytes 17154048 | tf_op jit(solution)/shard_map/dot_general | solution.py:59
  308.6 7.3 %multiply_convert_fusion = bf16[2048,384]{1,0:T(8,128)(2,1)S(1)} fusion(f32[2048,384]{1,0:T(8,128)S(1)} %fusion.3, bf16[2048,2880]{1,0:T(8,128)(2,1)S(1)} %bitcast.72, bf16[1,2880,384]{2,1,0:T(8,128)(2,1)S(1)} %copy-done.8), kind=kOutput, calls=%fused_computation.3 | convolution fusion | flops 4536139776 | bytes 18726912 | tf_op jit(solution)/shard_map/dot_general | solution.py:60
  315.9 11.4 %fusion.1 = f32[32,64,2880]{2,1,0:T(8,128)} fusion(bf16[32,64,384]{2,1,0:T(8,128)(2,1)S(1)} %bitcast.61, bf16[1,384,2880]{1,2,0:T(8,128)(2,1)S(1)} %copy-done), kind=kOutput, calls=%fused_computation.5 | convolution fusion | flops 4529848320 | bytes 27377664 | tf_op jit(solution)/shard_map/dot_general | solution.py:62
  327.3 213.4 %reduce-scatter.5.cloned.1.call-done = f32[8,64,2880]{2,1,0:T(8,128)} async-done(((f32[32,64,2880]{2,1,0:T(8,128)}), f32[8,64,2880]{2,1,0:T(8,128)}) %reduce-scatter.5.cloned.1.call-update) | async-done | bytes 5898256 | tf_op jit(solution)/shard_map/reduce_scatter | solution.py:123
  540.7 4.8 convert_element_type.48
  545.4 4.7 all-to-all-start.1
  550.3 68.6 %all-to-all-done.1 = bf16[8,64,2880]{2,1,0:T(8,128)(2,1)S(1)} async-done(((bf16[8,64,2880]{2,1,0:T(8,128)(2,1)}), bf16[8,64,2880]{2,1,0:T(8,128)(2,1)S(1)}, u32[]{:S(2)}, u32[]{:S(2)}) %all-to-all-start.1) | async-done | bytes 2949152 | tf_op jit(solution)/shard_map/all_to_all | solution.py:129
  618.9 2.7 gather_fusion
  621.5 4.1 reshape.116
  625.6 4.0 multiply_reduce_fusion
  629.6 0.9 add_convert_fusion
  (45 shorter events, 1.3 us)
Async XLA Ops:
  6.5 309.3 %copy-start = (bf16[1,384,2880]{1,2,0:T(8,128)(2,1)S(1)}, bf16[1,384,2880]{1,2,0:T(8,128)(2,1)}, u32[]{:S(2)}) copy-start(bf16[1,384,2880]{1,2,0:T(8,128)(2,1)} %param.21) | copy-start | bytes 6635524
  6.5 72.2 %all-gather.3.cloned.1.call-start = ((), (), s32[]{:S(2)}) async-start(), calls=%async_computation.4 | async-start | bytes 7372800 | tf_op jit(solution)/shard_map/all_gather | solution.py:95
  7.3 86.6 %reduce-scatter.3.cloned.1.call-start = ((), (), s32[]{:S(2)}) async-start(), calls=%async_computation.5 | async-start | bytes 2260992 | tf_op jit(solution)/shard_map/reduce_scatter | solution.py:98
  8.8 6.8 %collective-permute-start = (bf16[128,256]{1,0:T(8,128)(2,1)S(1)}, bf16[128,256]{1,0:T(8,128)(2,1)S(1)}, u32[]{:S(2)}, u32[]{:S(2)}) collective-permute-start(bf16[128,256]{1,0:T(8,128)(2,1)S(1)} %constant_dynamic-update-slice_fusion), channel_id=1, source_target_pairs={{0,2},{2,4},{4,6},{6,8},{8,10},{10,12},{12,14},{14,16},{16,18},{18... | collective-permute-start | bytes 196616 | tf_op jit(solution)/shard_map/ppermute | solution.py:19
  78.7 6.1 copy-start.5
  78.7 15.1 %copy-start.3 = (bf16[64,2880]{1,0:T(8,128)(2,1)S(1)}, bf16[64,2880]{1,0:T(8,128)(2,1)}, u32[]{:S(2)}) copy-start(bf16[64,2880]{1,0:T(8,128)(2,1)} %param.14) | copy-start | bytes 1105924
  84.7 10.5 %copy-start.4 = (f32[2880]{0:T(1024)S(1)}, f32[2880]{0:T(1024)}, u32[]{:S(2)}) copy-start(f32[2880]{0:T(1024)} %param.16) | copy-start | bytes 34564
  84.7 213.3 %all-gather.5.cloned.1.call-start = ((), (), s32[]{:S(2)}) async-start(), calls=%async_computation.6 | async-start | bytes 15073280 | tf_op jit(solution)/shard_map/all_gather | solution.py:119
  180.9 359.7 %reduce-scatter.5.cloned.1.call-start = ((), (), s32[]{:S(2)}) async-start(), calls=%async_computation.7 | async-start | bytes 30146560 | tf_op jit(solution)/shard_map/reduce_scatter | solution.py:123
  298.0 10.6 %copy-start.7 = (bf16[32,64,2880]{2,1,0:T(8,128)(2,1)S(1)}, bf16[32,64,2880]{2,1,0:T(8,128)(2,1)}, u32[]{:S(2)}) copy-start(bf16[32,64,2880]{2,1,0:T(8,128)(2,1)} %all-gather.5.cloned.1.call-done) | copy-start | bytes 35389444
  298.0 10.6 %copy-start.8 = (bf16[1,2880,384]{2,1,0:T(8,128)(2,1)S(1)}, bf16[1,2880,384]{2,1,0:T(8,128)(2,1)}, u32[]{:S(2)}) copy-start(bf16[1,2880,384]{2,1,0:T(8,128)(2,1)} %param.20) | copy-start | bytes 6635524
  545.4 4.7 copy-start.6
  545.4 73.4 %all-to-all-start.1 = ((bf16[8,64,2880]{2,1,0:T(8,128)(2,1)}), bf16[8,64,2880]{2,1,0:T(8,128)(2,1)S(1)}, u32[]{:S(2)}, u32[]{:S(2)}) async-start(bf16[8,64,2880]{2,1,0:T(8,128)(2,1)} %convert_element_type.48), calls=%async_computation.3 | async-start | bytes 6029312 | tf_op jit(solution)/shard_map/all_to_all | solution.py:129
  621.5 8.9 %copy-start.1 = (bf16[1,384,2880]{1,2,0:T(8,128)(2,1)S(1)}, bf16[1,384,2880]{1,2,0:T(8,128)(2,1)}, u32[]{:S(2)}) copy-start(bf16[1,384,2880]{1,2,0:T(8,128)(2,1)} %param.21) | copy-start | bytes 6635524
  625.6 4.0 copy-start.2
Sparse Core Ops, SparseCore 0:
  9.2 69.4 all-gather.2
  84.8 8.9 reduce-scatter.2
  181.0 116.8 all-gather.4
  327.4 213.2 reduce-scatter.4
where the time goes:
time: 638 us; the launch traced here: 637 us
  waiting for transfers between devices  469 us (74%)
  blocking collectives  73.8 us (12%)
  matrix products  37.1 us (6%)
  local copies, waits for them, and re-layouts  21.2 us (3%)
  between operations  13.3 us (2%)
  other arithmetic  13.1 us (2%)
  starting transfers between devices  9.91 us (2%)
    reduce_scatter x1, waiting for transfers between devices, local(): lax.psum_scatter(partial_rows.reshape(experts * lax.axis_size('exp'), cap...  213 us
    all_gather x1, waiting for transfers between devices, local(): pooled = lax.all_gather(arrived, 'exp', axis=0, tiled=True)  117 us
    all_to_all x1, blocking collectives, local(): lax.all_to_all(outgoing, ('ctx', 'head'), split_axis=0, concat_axis=0, ti...  73.8 us
    all_to_all x1, waiting for transfers between devices, local(): lax.all_to_all(summed, ('ctx', 'head'), split_axis=0, concat_axis=0, tile...  68.6 us
    all_gather x1, waiting for transfers between devices, local(): lax.all_gather(out_projection, 'exp', axis=1, tiled=True)  61 us
  transfers between devices with their start and end apart: 6, of which 6 were waited for; matrix products, arithmetic and copies ran while one was open for 1% of the time, Pallas kernels for 0%

commit v1 on v0

--- a/solution.py
+++ b/solution.py
@@ -116,7 +116,21 @@
     )
     outgoing = outgoing.reshape(experts, capacity, D)
     arrived = lax.all_to_all(outgoing, ("ctx", "head"), split_axis=0, concat_axis=0, tiled=True)
-    pooled = lax.all_gather(arrived, "exp", axis=0, tiled=True)
+    ways, here, turn = (lax.axis_size("exp"), lax.axis_index("exp"), arrived.shape[0])
+    lengths = [n * ways if d == 0 else n for d, n in enumerate(arrived.shape)]
+    full = lax.dynamic_update_slice_in_dim(
+        jnp.zeros(lengths, arrived.dtype), arrived, here * turn, axis=0
+    )
+    going_up = going_down = arrived
+    for far in range(1, ways // 2 + 1):
+        going_up = lax.ppermute(going_up, "exp", [(d, (d + 1) % ways) for d in range(ways)])
+        full = lax.dynamic_update_slice_in_dim(full, going_up, (here - far) % ways * turn, axis=0)
+        if 2 * far < ways:
+            going_down = lax.ppermute(going_down, "exp", [(d, (d - 1) % ways) for d in range(ways)])
+            full = lax.dynamic_update_slice_in_dim(
+                full, going_down, (here + far) % ways * turn, axis=0
+            )
+    pooled = full
     partial_rows = expert_rows(
         pooled.reshape(experts * lax.axis_size("exp") * capacity, D), w_gate[0], w_up[0], w_down[0]
     )

time: 638 us -> 724 us (1.13)
  waiting for transfers between devices: 469 us -> 527 us
  local copies, waits for them, and re-layouts: 21.2 us -> 45.6 us
    ppermute x0 -> x3, waiting for transfers between devices: none -> 177 us  [the longest x2 126 us: local(): lax.ppermute(going_up, 'exp', [(d, (d + 1) % ways) for d in range(ways)])]
    all_gather x1 -> x0, waiting for transfers between devices: 117 us -> none  [local(): pooled = lax.all_gather(arrived, 'exp', axis=0, tiled=True)]
    dynamic_update_slice x0 -> x4, local copies, waits for them, and re-layouts: none -> 14.8 us  [the longest x2 7.41 us: local(): lax.dynamic_update_slice_in_dim(full, going_up, (here - far) % ways * tur...]
  transfers between devices with their start and end apart: 6 -> 8, of which waited for: 6 -> 8; matrix products, arithmetic and copies ran while one was open for 1% -> 3% of each run, Pallas kernels for 0% -> 0%
where the time goes in v1:
time: 724 us; the launch traced here: 723 us
  waiting for transfers between devices  527 us (73%)
  blocking collectives  73.8 us (10%)
  local copies, waits for them, and re-layouts  45.6 us (6%)
  matrix products  37.4 us (5%)
  between operations  13.3 us (2%)
  starting transfers between devices  13.2 us (2%)
  other arithmetic  13.2 us (2%)
    reduce_scatter x1, waiting for transfers between devices, local(): lax.psum_scatter(partial_rows.reshape(experts * lax.axis_size('exp'), cap...  212 us
    ppermute x2, waiting for transfers between devices, local(): lax.ppermute(going_up, 'exp', [(d, (d + 1) % ways) for d in range(ways)])  126 us
    all_to_all x1, blocking collectives, local(): lax.all_to_all(outgoing, ('ctx', 'head'), split_axis=0, concat_axis=0, ti...  73.8 us
    all_to_all x1, waiting for transfers between devices, local(): lax.all_to_all(summed, ('ctx', 'head'), split_axis=0, concat_axis=0, tile...  68.6 us
    all_gather x1, waiting for transfers between devices, local(): lax.all_gather(out_projection, 'exp', axis=1, tiled=True)  61 us
    ppermute x1, waiting for transfers between devices, local(): lax.ppermute(going_down, 'exp', [(d, (d - 1) % ways) for d in range(ways)])  50.7 us
  transfers between devices with their start and end apart: 8, of which 8 were waited for; matrix products, arithmetic and copies ran while one was open for 3% of the time, Pallas kernels for 0%

profile of v1, /device:TPU:0, one launch (start us, length us, event | category | flops | bytes accessed | tf_op | source)
XLA Modules:
  0.0 723.4 jit_solution(2656331731684412705)
XLA Ops:
  8.8 4.9 collective-permute-start
  13.9 1.1 copy.19
  16.6 1.1 convolution_convert_fusion
  17.7 61.0 %all-gather.2.cloned.1.call-done = bf16[1024,2880]{0,1:T(8,128)(2,1)} async-done(((bf16[1024,720]{0,1:T(8,128)(2,1)}), bf16[1024,2880]{0,1:T(8,128)(2,1)}) %all-gather.2.cloned.1.call-update) | async-done | bytes 5898256 | tf_op jit(solution)/shard_map/all_gather | solution.py:95
  78.7 6.0 fusion.30
  86.2 7.6 %reduce-scatter.3.cloned.1.call-done = f32[64,2880]{1,0:T(8,128)} async-done(((f32[128,2880]{1,0:T(8,128)}), f32[64,2880]{1,0:T(8,128)}) %reduce-scatter.3.cloned.1.call-update) | async-done | bytes 737296 | tf_op jit(solution)/shard_map/reduce_scatter | solution.py:98
  93.8 1.3 multiply_reduce_fusion.1
  95.2 1.3 multiply_convert_fusion.1
  96.4 1.5 broadcast_in_dim.42
  98.0 3.6 reshape.129
  101.5 5.6 scatter_custom_fusion
  107.1 73.8 %all_to_all.10 = bf16[8,64,2880]{2,1,0:T(8,128)(2,1)} all-to-all(bf16[8,64,2880]{2,1,0:T(8,128)(2,1)} %bitcast.63), channel_id=1, replica_groups=mesh['ctx'=4,'exp'=4,'head'=2] {'ctx','head'}, dimensions={0} | all-to-all | bytes 5898240 | tf_op jit(solution)/shard_map/all_to_all | solution.py:118
  180.9 1.5 collective-permute-start.1
  182.4 1.5 collective-permute-start.2
  183.8 66.5 %collective-permute-done.1 = bf16[8,64,2880]{2,1,0:T(8,128)(2,1)} collective-permute-done((bf16[8,64,2880]{2,1,0:T(8,128)(2,1)}, bf16[8,64,2880]{2,1,0:T(8,128)(2,1)}, u32[]{:S(2)}, u32[]{:S(2)}) %collective-permute-start.1) | collective-permute-done | bytes 2949152 | tf_op jit(solution)/shard_map/ppermute | solution.py:126
  250.8 6.1 broadcast_in_dim.40
  256.9 3.7 constant_dynamic-update-slice_fusion.5
  260.6 3.7 constant_dynamic-update-slice_fusion.4
  264.2 50.7 %collective-permute-done.2 = bf16[8,64,2880]{2,1,0:T(8,128)(2,1)} collective-permute-done((bf16[8,64,2880]{2,1,0:T(8,128)(2,1)}, bf16[8,64,2880]{2,1,0:T(8,128)(2,1)}, u32[]{:S(2)}, u32[]{:S(2)}) %collective-permute-start.2) | collective-permute-done | bytes 2949152 | tf_op jit(solution)/shard_map/ppermute | solution.py:129
  314.9 3.7 constant_dynamic-update-slice_fusion.3
  318.6 59.5 %collective-permute-done.3 = bf16[8,64,2880]{2,1,0:T(8,128)(2,1)} collective-permute-done((bf16[8,64,2880]{2,1,0:T(8,128)(2,1)}, bf16[8,64,2880]{2,1,0:T(8,128)(2,1)}, u32[]{:S(2)}, u32[]{:S(2)}) %collective-permute-start.3) | collective-permute-done | bytes 2949152 | tf_op jit(solution)/shard_map/ppermute | solution.py:126
  378.2 3.7 constant_dynamic-update-slice_fusion.2
  381.9 10.8 %fusion.7 = f32[2048,384]{1,0:T(8,128)S(1)} fusion(bf16[2048,2880]{1,0:T(8,128)(2,1)} %bitcast.61, bf16[1,2880,384]{2,1,0:T(8,128)(2,1)S(1)} %copy-done.7), kind=kOutput, calls=%fused_computation.9 | convolution fusion | flops 4529848320 | bytes 17154048 | tf_op jit(solution)/shard_map/dot_general | solution.py:60
  392.7 7.4 %multiply_convert_fusion = bf16[2048,384]{1,0:T(8,128)(2,1)S(1)} fusion(f32[2048,384]{1,0:T(8,128)S(1)} %fusion.7, bf16[2048,2880]{1,0:T(8,128)(2,1)S(1)} %bitcast.62, bf16[1,2880,384]{2,1,0:T(8,128)(2,1)S(1)} %copy-done.8), kind=kOutput, calls=%fused_computation.3 | convolution fusion | flops 4536139776 | bytes 18726912 | tf_op jit(solution)/shard_map/dot_general | solution.py:59
  400.2 11.4 %fusion.1 = f32[32,64,2880]{2,1,0:T(8,128)} fusion(bf16[32,64,384]{2,1,0:T(8,128)(2,1)S(1)} %bitcast.64, bf16[1,384,2880]{1,2,0:T(8,128)(2,1)S(1)} %copy-done), kind=kOutput, calls=%fused_computation.5 | convolution fusion | flops 4529848320 | bytes 27377664 | tf_op jit(solution)/shard_map/dot_general | solution.py:62
  411.6 211.7 %reduce-scatter.5.cloned.1.call-done = f32[8,64,2880]{2,1,0:T(8,128)} async-done(((f32[32,64,2880]{2,1,0:T(8,128)}), f32[8,64,2880]{2,1,0:T(8,128)}) %reduce-scatter.5.cloned.1.call-update) | async-done | bytes 5898256 | tf_op jit(solution)/shard_map/reduce_scatter | solution.py:137
  623.3 4.8 convert_element_type.48
  628.1 4.8 all-to-all-start.1
  633.0 68.6 %all-to-all-done.1 = bf16[8,64,2880]{2,1,0:T(8,128)(2,1)} async-done(((bf16[8,64,2880]{2,1,0:T(8,128)(2,1)}), bf16[8,64,2880]{2,1,0:T(8,128)(2,1)}, u32[]{:S(2)}, u32[]{:S(2)}) %all-to-all-start.1) | async-done | bytes 2949152 | tf_op jit(solution)/shard_map/all_to_all | solution.py:143
  701.7 6.4 gather_fusion
  708.1 3.9 reshape.116
  712.0 4.0 multiply_reduce_fusion
  (53 shorter events, 7.1 us)
Async XLA Ops:
  6.5 393.6 %copy-start = (bf16[1,384,2880]{1,2,0:T(8,128)(2,1)S(1)}, bf16[1,384,2880]{1,2,0:T(8,128)(2,1)}, u32[]{:S(2)}) copy-start(bf16[1,384,2880]{1,2,0:T(8,128)(2,1)} %param.21) | copy-start | bytes 6635524
  6.5 72.2 %all-gather.2.cloned.1.call-start = ((), (), s32[]{:S(2)}) async-start(), calls=%async_computation.4 | async-start | bytes 7372800 | tf_op jit(solution)/shard_map/all_gather | solution.py:95
  7.3 86.6 %reduce-scatter.3.cloned.1.call-start = ((), (), s32[]{:S(2)}) async-start(), calls=%async_computation.5 | async-start | bytes 2260992 | tf_op jit(solution)/shard_map/reduce_scatter | solution.py:98
  8.8 6.8 collective-permute-start
  78.7 6.1 copy-start.5
  78.7 15.1 %copy-start.3 = (bf16[64,2880]{1,0:T(8,128)(2,1)S(1)}, bf16[64,2880]{1,0:T(8,128)(2,1)}, u32[]{:S(2)}) copy-start(bf16[64,2880]{1,0:T(8,128)(2,1)} %param.14) | copy-start | bytes 1105924
  78.7 16.5 %copy-start.4 = (f32[2880]{0:T(1024)S(1)}, f32[2880]{0:T(1024)}, u32[]{:S(2)}) copy-start(f32[2880]{0:T(1024)} %param.16) | copy-start | bytes 34564
  84.7 538.6 %reduce-scatter.5.cloned.1.call-start = ((), (), s32[]{:S(2)}) async-start(), calls=%async_computation.6 | async-start | bytes 30146560 | tf_op jit(solution)/shard_map/reduce_scatter | solution.py:137
  180.9 69.4 %collective-permute-start.1 = (bf16[8,64,2880]{2,1,0:T(8,128)(2,1)}, bf16[8,64,2880]{2,1,0:T(8,128)(2,1)}, u32[]{:S(2)}, u32[]{:S(2)}) collective-permute-start(bf16[8,64,2880]{2,1,0:T(8,128)(2,1)} %all_to_all.10), channel_id=1, source_target_pairs={{0,2},{2,4},{4,6},{6,0},{1,3},{3,5},{5,7},{7,1},{8,10},{10,12},{12... | collective-permute-start | bytes 8847368 | tf_op jit(solution)/shard_map/ppermute | solution.py:126
  182.4 132.5 %collective-permute-start.2 = (bf16[8,64,2880]{2,1,0:T(8,128)(2,1)}, bf16[8,64,2880]{2,1,0:T(8,128)(2,1)}, u32[]{:S(2)}, u32[]{:S(2)}) collective-permute-start(bf16[8,64,2880]{2,1,0:T(8,128)(2,1)} %all_to_all.10), channel_id=1, source_target_pairs={{0,6},{2,0},{4,2},{6,4},{1,7},{3,1},{5,3},{7,5},{8,14},{10,8},{12,... | collective-permute-start | bytes 8847368 | tf_op jit(solution)/shard_map/ppermute | solution.py:129
  250.3 127.9 %collective-permute-start.3 = (bf16[8,64,2880]{2,1,0:T(8,128)(2,1)}, bf16[8,64,2880]{2,1,0:T(8,128)(2,1)}, u32[]{:S(2)}, u32[]{:S(2)}) collective-permute-start(bf16[8,64,2880]{2,1,0:T(8,128)(2,1)} %collective-permute-done.1), channel_id=1, source_target_pairs={{0,2},{2,4},{4,6},{6,0},{1,3},{3,5},{5,7},{7,1},{8,10},{10,12},{12... | collective-permute-start | bytes 8847368 | tf_op jit(solution)/shard_map/ppermute | solution.py:126
  318.6 63.3 %copy-start.7 = (bf16[1,2880,384]{2,1,0:T(8,128)(2,1)S(1)}, bf16[1,2880,384]{2,1,0:T(8,128)(2,1)}, u32[]{:S(2)}) copy-start(bf16[1,2880,384]{2,1,0:T(8,128)(2,1)} %param.20) | copy-start | bytes 6635524
  381.9 10.8 %copy-start.1 = (bf16[32,64,2880]{2,1,0:T(8,128)(2,1)S(1)}, bf16[32,64,2880]{2,1,0:T(8,128)(2,1)}, u32[]{:S(2)}) copy-start(bf16[32,64,2880]{2,1,0:T(8,128)(2,1)} %constant_dynamic-update-slice_fusion.2) | copy-start | bytes 35389444
  381.9 10.8 %copy-start.8 = (bf16[1,2880,384]{2,1,0:T(8,128)(2,1)S(1)}, bf16[1,2880,384]{2,1,0:T(8,128)(2,1)}, u32[]{:S(2)}) copy-start(bf16[1,2880,384]{2,1,0:T(8,128)(2,1)} %param.19) | copy-start | bytes 6635524
  628.1 4.8 copy-start.6
  628.1 73.5 %all-to-all-start.1 = ((bf16[8,64,2880]{2,1,0:T(8,128)(2,1)}), bf16[8,64,2880]{2,1,0:T(8,128)(2,1)}, u32[]{:S(2)}, u32[]{:S(2)}) async-start(bf16[8,64,2880]{2,1,0:T(8,128)(2,1)} %convert_element_type.48), calls=%async_computation.3 | async-start | bytes 6029312 | tf_op jit(solution)/shard_map/all_to_all | solution.py:143
  712.0 4.0 copy-start.2
Sparse Core Ops, SparseCore 0:
  9.2 69.4 all-gather.1
  84.8 8.9 reduce-scatter.2
  411.7 211.5 reduce-scatter.4
